TPU v7x, 32 devices: a whole 2x2x4 slice. The times are simulated.
32 devices in a mesh: seq: 8 (over y, x, core), head: 4 (over z).
Axes of the slice: x: 2, y: 2, z: 4, core: 2. Of those that a mesh axis runs over, the one named last changes fastest.
Arguments:
- queries: bfloat16 [3, 2048, 2048], P(None, 'seq', 'head'), may hold values from -24 to 24
- key_vectors: bfloat16 [4, 2048, 2048], P(None, 'seq', 'head'), may hold values from -24 to 24
- values: bfloat16 [4, 2048, 2048], P(None, 'seq', 'head'), may hold values from -6 to 6
- learn_rates: float32 [3, 2048, 4], P(None, 'seq', 'head'), may hold values from 0.001 to 0.01
- norm_gain: float32 [2048], P('head'), may hold values from 0.1 to 1.9
- out_weight: bfloat16 [2048, 2048], P('head'), may hold values from -0.125 to 0.125
- incoming: float32 [8, 4, 3, 512, 512], P('seq', 'head'), may hold values from -0.25 to 0.25
Outputs:
- mixed_out: bfloat16 [3, 2048, 2048], P(None, 'seq', 'head')
- outgoing: float32 [8, 4, 3, 512, 512], P('seq', 'head')
All inputs are finite; a program needn't handle non-finite values.
Results may differ from a plain program's by a relative error of at most 0.013.
The roundings to bfloat16 on the way count: a program that leaves them out, or rounds other values in their place, can miss the bound.
Values may be sent and summed in bfloat16 or wider, within the bound.
A program may use at most 64 MiB of HBM per device.

v0:
```python
import functools

import jax
import jax.numpy as jnp
from jax import lax
from jax.experimental import pallas as pl
from jax.experimental.pallas import tpu as pltpu
from jax.sharding import PartitionSpec as P


F32, BF16 = jnp.float32, jnp.bfloat16


def shifted(x, axis, by):
    count = lax.axis_size(axis)
    return lax.ppermute(x, axis, [(i, (i + by) % count) for i in range(count)])


def dot(a, b, over=(1, 0)):
    return lax.dot_general(a, b, (((over[0],), (over[1],)), ((), ())), preferred_element_type=F32)


def normed_apply(rounded, query_rows, gain_row):
    first_proj = dot(query_rows, rounded[0])
    third_proj = dot(query_rows, rounded[1])
    hidden = (first_proj * jax.nn.sigmoid(first_proj) * third_proj).astype(BF16)
    fast_out = dot(hidden, rounded[2])
    mean_sq = jnp.mean(fast_out * fast_out, axis=1, keepdims=True)
    return fast_out * lax.rsqrt(mean_sq + 1e-06) * gain_row


def fast_update(olds, rounded, key_rows, scaled_values, stores):
    first_proj = dot(key_rows, rounded[0])
    third_proj = dot(key_rows, rounded[1])
    gate_sig = jax.nn.sigmoid(first_proj)
    gated = first_proj * gate_sig

    def put(i, grad):
        old = olds[i]()
        stepped = old + grad
        before_sq = jnp.mean(old * old, axis=0, keepdims=True)
        after_sq = jnp.mean(stepped * stepped, axis=0, keepdims=True)
        stores[i](stepped * jnp.sqrt((before_sq + 1e-06) / (after_sq + 1e-06)))

    hidden = (gated * third_proj).astype(BF16)
    back_grad = dot(scaled_values, rounded[2], (1, 1))
    put(2, dot(hidden, scaled_values, (0, 0)))
    slope = gate_sig * (1.0 + first_proj * (1.0 - gate_sig))
    put(0, dot(key_rows, (back_grad * third_proj * slope).astype(BF16), (0, 0)))
    put(1, dot(key_rows, (back_grad * gated).astype(BF16), (0, 0)))


def attend(query_rows, prior_keys, own_keys, prior_vals, own_vals):
    length, size = query_rows.shape
    row = lax.broadcasted_iota(jnp.int32, (length, length), 0)
    own = lax.broadcasted_iota(jnp.int32, (length, length), 1) <= row
    scores = jnp.where(
        own, dot(query_rows, own_keys, (1, 1)), dot(query_rows, prior_keys, (1, 1))
    ) * size ** (-0.5)
    expo = jnp.exp(scores - jnp.max(scores, axis=1, keepdims=True))
    probs = expo / jnp.sum(expo, axis=1, keepdims=True)
    zero = jnp.zeros_like(probs)
    own_probs = jnp.where(own, probs, zero).astype(BF16)
    prior_probs = jnp.where(own, zero, probs).astype(BF16)
    return dot(own_probs, own_vals) + dot(prior_probs, prior_vals)


def scaled(rate_rows, vals):
    return (rate_rows * vals.astype(F32)).astype(BF16)


def project(combined, weight_ref, keep_ref, send_ref):
    count = lax.axis_size("head")
    me = lax.axis_index("head")
    width = weight_ref.shape[1] // count
    for step in range(count):
        place, slot = divmod(step, 2)
        target = lax.rem(me, 2)
        target = (1 - target if place else target) + 2 * (
            lax.div(me, 2) if slot == 0 else 1 - lax.div(me, 2)
        )
        columns = pl.ds(pl.multiple_of(target * width, 128), width)
        piece = dot(combined, weight_ref[:, columns]).astype(BF16)
        out = send_ref if place else keep_ref
        out[:, slot * width : (slot + 1) * width] = piece


def split_kernel(q_ref, key0, key1, key2, val0, val1, val2, q_out, near0, near1, near2):
    q_out[...] = q_ref[0]
    for out, k_ref, v_ref in ((near0, key0, val0), (near1, key1, val1), (near2, key2, val2)):
        out[0] = k_ref[0]
        out[1] = v_ref[0]


def first_kernel(old_ref, key_ref, val_ref, rate_ref, sent_ref):
    def store(i, x):
        sent_ref[i] = x.astype(BF16)

    fast_update(
        [lambda i=i: old_ref[0, 0, i] for i in range(3)],
        [old_ref[0, 0, i].astype(BF16) for i in range(3)],
        key_ref[0],
        scaled(rate_ref[0], val_ref[0]),
        [functools.partial(store, i) for i in range(3)],
    )


def window_of(near_ref, q_ref, k_ref, v_ref):
    return attend(q_ref[0], near_ref[0], k_ref[0], near_ref[1], v_ref[0])


def mix_first_kernel(old_ref, near_ref, q_ref, k_ref, v_ref, gain_ref, w_ref, keep, send):
    rounded = [old_ref[0, 0, i].astype(BF16) for i in range(3)]
    normed = normed_apply(rounded, q_ref[0], gain_ref[...])
    att = window_of(near_ref, q_ref, k_ref, v_ref)
    project((att + normed).astype(BF16), w_ref, keep, send)


def apply_kernel(held_ref, q_ref, gain_ref, out_ref):
    rounded = [held_ref[i] for i in range(3)]
    out_ref[...] = normed_apply(rounded, q_ref[...], gain_ref[...]).astype(BF16)


def mix_kernel(normed_ref, near_ref, q_ref, k_ref, v_ref, w_ref, keep, send):
    att = window_of(near_ref, q_ref, k_ref, v_ref)
    project((att + normed_ref[...].astype(F32)).astype(BF16), w_ref, keep, send)


def attend_kernel(near_ref, q_ref, k_ref, v_ref, out_ref):
    out_ref[...] = window_of(near_ref, q_ref, k_ref, v_ref)


def middle_kernel(
    held_ref, near_ref, rate_ref, q_ref, gain_ref, att_ref, w_ref, state_ref, *halves
):
    def store(i, x):
        state_ref[i] = x

    fast_update(
        [lambda i=i: held_ref[i].astype(F32) for i in range(3)],
        [held_ref[i] for i in range(3)],
        near_ref[0],
        scaled(rate_ref[...], near_ref[1]),
        [functools.partial(store, i) for i in range(3)],
    )
    rounded = [state_ref[i].astype(BF16) for i in range(3)]
    normed = normed_apply(rounded, q_ref[0], gain_ref[...])
    combined = (att_ref[...] + normed).astype(BF16)
    rows = halves[0].shape[0]
    for at_row in range(0, combined.shape[0], rows):
        keep, send = halves[2 * (at_row // rows) :][:2]
        project(combined[at_row : at_row + rows], w_ref, keep, send)


def last_kernel(old_ref, key_ref, val_ref, rate_ref, out_ref):
    def store(i, x):
        out_ref[0, 0, i] = x

    fast_update(
        [lambda i=i: old_ref[i] for i in range(3)],
        [old_ref[i].astype(BF16) for i in range(3)],
        key_ref[0],
        scaled(rate_ref[0], val_ref[0]),
        [functools.partial(store, i) for i in range(3)],
    )


def whole(x):
    return pl.BlockSpec(x.shape, lambda i: (0,) * len(x.shape))


def at(x, index):
    return pl.BlockSpec((1,) + x.shape[1:], lambda i: (index,) + (0,) * (len(x.shape) - 1))


def call(kernel, args, outs, flops):
    arrays = [a[0] if isinstance(a, tuple) else a for a in args]
    specs = [at(*a) if isinstance(a, tuple) else whole(a) for a in args]
    shapes = [jax.ShapeDtypeStruct(s, t) for s, t in outs]
    got = pl.pallas_call(
        kernel,
        out_shape=shapes,
        grid=(1,),
        in_specs=specs,
        out_specs=[whole(s) for s in shapes],
        compiler_params=pltpu.CompilerParams(vmem_limit_bytes=40 << 20),
        cost_estimate=pl.CostEstimate(flops=flops, bytes_accessed=4 << 20, transcendentals=0),
    )(*arrays)
    return got


def pair_sum(keep, send):
    count = lax.axis_size("head")
    got = lax.ppermute(send, "head", [(i, i ^ 1) for i in range(count)])
    pair = keep.astype(F32) + got.astype(F32)
    width = keep.shape[1] // 2
    return pair[:, :width], pair[:, width:].astype(BF16)


def last_sum(own, far):
    count = lax.axis_size("head")
    got = lax.ppermute(far, "head", [(i, i ^ 2) for i in range(count)])
    return (own + got.astype(F32)).astype(BF16)


def layer(queries, key_vectors, values, learn_rates, norm_gain, out_weight, incoming):
    ticks, rows, size = queries.shape
    last = ticks - 1
    unit = 2 * rows * size * size
    gain_row = norm_gain[None, :]
    wide = out_weight.shape[1] // 2
    half, quarter = ((rows, wide), BF16), ((rows // 2, wide), BF16)
    both = ((2, rows, size), BF16)
    block = ((rows, size), BF16)

    rate_near = shifted(learn_rates[1].reshape(1, -1), "seq", 1).reshape(-1, 1)
    ahead, near0, near1, near2 = call(
        split_kernel,
        [(queries, 1)] + [(key_vectors, t) for t in range(3)] + [(values, t) for t in range(3)],
        [block, both, both, both],
        0,
    )
    ahead = shifted(ahead, "seq", -1)
    near0 = shifted(near0, "seq", 1)
    near1 = shifted(near1, "seq", 1)

    def window(t):
        return [(queries, t), (key_vectors, t + 1), (values, t + 1)]

    (sent,) = call(
        first_kernel,
        [incoming, (key_vectors, 1), (values, 1), (learn_rates, 0)],
        [((3, size, size), BF16)],
        6 * unit,
    )
    (normed_far,) = call(apply_kernel, [sent, ahead, gain_row], [block], 3 * unit)
    normed = shifted(normed_far, "seq", 1)
    near2 = shifted(near2, "seq", 1)
    held = shifted(sent, "seq", last)
    near0, rate_near = lax.optimization_barrier((near0, rate_near))
    sums = [
        pair_sum(
            *call(mix_first_kernel, [incoming, near0, *window(0), gain_row, out_weight], [half] * 2, 9 * unit)
        )
    ]
    sums.append(pair_sum(*call(mix_kernel, [normed, near1, *window(1), out_weight], [half] * 2, 6 * unit)))
    (att,) = call(attend_kernel, [near2, *window(2)], [((rows, size), F32)], 2 * unit)
    state, *halves = call(
        middle_kernel,
        [held, near2, rate_near, (queries, 2), gain_row, att, out_weight],
        [((3, size, size), F32)] + [quarter] * 4,
        13 * unit,
    )
    outputs = [last_sum(*pair) for pair in sums]
    lower = last_sum(*pair_sum(*halves[:2]))
    upper = last_sum(*pair_sum(*halves[2:]))
    outputs.append(jnp.concatenate([lower, upper], axis=0))
    (outgoing,) = call(
        last_kernel, [state, (key_vectors, 3), (values, 3), (learn_rates, 2)], [(incoming.shape, F32)], 6 * unit
    )
    return (jnp.stack(outputs), outgoing)


def solution(mesh):
    placed = (
        P(None, "seq", "head"),
        P(None, "seq", "head"),
        P(None, "seq", "head"),
        P(None, "seq", "head"),
        P("head"),
        P("head", None),
        P("seq", "head", None, None, None),
    )
    return jax.shard_map(
        layer,
        mesh=mesh,
        in_specs=placed,
        out_specs=(P(None, "seq", "head"), P("seq", "head", None, None, None)),
        check_vma=False,
    )
```

profile of v0, /device:TPU:0, one launch (start us, length us, event | category | flops | bytes accessed | tf_op | source)
XLA Modules:
  0.0 131.8 jit_solution(17362745369931668754)
XLA Ops:
  0.6 0.0 copy-start
  0.6 1.2 copy-done
  1.9 1.2 copy-done.2
  3.1 1.1 copy-done.6
  4.2 1.1 shard_map.86
  5.4 0.8 copy-done.15
  6.2 0.5 collective-permute-start
  6.7 2.9 %collective-permute-start.4 = (bf16[256,512]{1,0:T(8,128)(2,1)}, bf16[256,512]{1,0:T(8,128)(2,1)S(1)}, u32[]{:S(2)}, u32[]{:S(2)}) collective-permute-start(bf16[256,512]{1,0:T(8,128)(2,1)} %get-tuple-element.21), channel_id=1, source_target_pairs={{0,28},{4,0},{8,4},{12,8},{16,12},{20,16},{24,20},{28,24},{1,29},{... | collective-permute-start | bytes 786440 | tf_op jit(solution)/shard_map/ppermute | solution.py:16
  9.5 0.0 copy-done.17
  9.5 0.2 copy.11.rate_ref
  9.7 0.0 copy-done.1
  9.7 0.0 copy-done.3
  9.7 0.0 copy-start.4
  9.8 1.9 %copy-done.4 = f32[1,1,3,512,512]{4,3,2,1,0:T(8,128)S(1)} copy-done((f32[1,1,3,512,512]{4,3,2,1,0:T(8,128)S(1)}, f32[1,1,3,512,512]{4,3,2,1,0:T(8,128)}, u32[]{:S(2)}) %copy-start.4) | copy-done | bytes 3145752
  11.6 0.0 copy-start.8
  11.7 2.9 %shard_map.88.held_ref = bf16[3,512,512]{2,1,0:T(8,128)(2,1)} custom-call(f32[1,1,3,512,512]{4,3,2,1,0:T(8,128)S(1)} %copy-done.4, bf16[4,256,512]{2,1,0:T(8,128)(2,1)S(1)} %copy-done.1, bf16[4,256,512]{2,1,0:T(8,128)(2,1)S(1)} %copy-done.3, f32[3,256,1]{2,1,0:T(8,128)S(1)} %copy.11.rate_ref), custom_call_target="tpu_custom_call" | custom-call | flops 805306368 | bytes 4194304 | tf_op jit(solution)/shard_map/pallas_call | solution.py:180
  14.6 1.3 %collective-permute-start.9 = (bf16[3,512,512]{2,1,0:T(8,128)(2,1)}, bf16[3,512,512]{2,1,0:T(8,128)(2,1)}, u32[]{:S(2)}, u32[]{:S(2)}) collective-permute-start(bf16[3,512,512]{2,1,0:T(8,128)(2,1)} %shard_map.88.held_ref), channel_id=1, source_target_pairs={{0,8},{4,12},{8,16},{12,20},{16,24},{20,28},{24,0},{28,4},{1,9},{5... | collective-permute-start | bytes 4718600 | tf_op jit(solution)/shard_map/ppermute | solution.py:16
  15.9 0.0 copy-done.16
  15.9 0.0 collective-permute-start.6
  15.9 2.5 %collective-permute-start.1 = (f32[1,256]{1,0:T(1,128)S(1)}, f32[1,256]{1,0:T(1,128)S(1)}, u32[]{:S(2)}, u32[]{:S(2)}) collective-permute-start(f32[1,256]{1,0:T(1,128)S(1)} %slice_bitcast_fusion), channel_id=1, source_target_pairs={{0,4},{4,8},{8,12},{12,16},{16,20},{20,24},{24,28},{28,0},{1,5},{5... | collective-permute-start | bytes 3080 | tf_op jit(solution)/shard_map/ppermute | solution.py:16
  18.5 0.0 collective-permute-done.4.q_ref
  18.5 0.1 collective-permute-start.10
  18.5 0.0 copy-done.14
  18.5 2.1 %shard_map.89 = bf16[256,512]{1,0:T(8,128)(2,1)S(1)} custom-call(bf16[3,512,512]{2,1,0:T(8,128)(2,1)} %shard_map.88.held_ref, bf16[256,512]{1,0:T(8,128)(2,1)S(1)} %collective-permute-done.4.q_ref, f32[1,512]{1,0:T(1,128)S(1)} %bitcast.10), custom_call_target="tpu_custom_call" | custom-call | flops 402653184 | bytes 4194304 | tf_op jit(solution)/shard_map/pallas_call | solution.py:180
  20.7 38.1 %collective-permute-done.1 = f32[1,256]{1,0:T(1,128)S(1)} collective-permute-done((f32[1,256]{1,0:T(1,128)S(1)}, f32[1,256]{1,0:T(1,128)S(1)}, u32[]{:S(2)}, u32[]{:S(2)}) %collective-permute-start.1) | collective-permute-done | bytes 1056 | tf_op jit(solution)/shard_map/ppermute | solution.py:16
  58.8 0.0 collective-permute-start.5
  58.8 0.0 collective-permute-done.near_ref
  58.8 0.0 copy-done.5
  58.8 0.0 copy-done.7
  58.8 3.7 %shard_map.87 = (bf16[256,1024]{1,0:T(8,128)(2,1)S(1)}, bf16[256,1024]{1,0:T(8,128)(2,1)}) custom-call(f32[1,1,3,512,512]{4,3,2,1,0:T(8,128)S(1)} %copy-done.5, bf16[2,256,512]{2,1,0:T(8,128)(2,1)} %collective-permute-done.near_ref, bf16[3,256,512]{2,1,0:T(8,128)(2,1)S(1)} %copy-done.7, bf16[4,256,512]{2,1,0:T(8,128)(2,1)S(1)} %copy-done.1, ...), custom_call_target="tpu_custom_call" | custom-call | flops 1207959552 | bytes 4194304 | tf_op jit(solution)/shard_map/pallas_call | solution.py:180
  62.5 2.3 %collective-permute-start.2 = (bf16[256,1024]{1,0:T(8,128)(2,1)}, bf16[256,1024]{1,0:T(8,128)(2,1)}, u32[]{:S(2)}, u32[]{:S(2)}) collective-permute-start(bf16[256,1024]{1,0:T(8,128)(2,1)} %get-tuple-element.20), channel_id=1, source_target_pairs={{0,1},{1,0},{2,3},{3,2},{4,5},{5,4},{6,7},{7,6},{8,9},{9,8},{10,11... | collective-permute-start | bytes 1572872 | tf_op jit(solution)/shard_map/ppermute | solution.py:194
  64.8 2.3 %collective-permute-done.5.normed_ref = bf16[256,512]{1,0:T(8,128)(2,1)S(1)} collective-permute-done((bf16[256,512]{1,0:T(8,128)(2,1)S(1)}, bf16[256,512]{1,0:T(8,128)(2,1)S(1)}, u32[]{:S(2)}, u32[]{:S(2)}) %collective-permute-start.5) | collective-permute-done | bytes 262176 | tf_op jit(solution)/shard_map/ppermute | solution.py:16
  67.2 0.0 collective-permute-done.6.near_ref
  67.2 2.2 %shard_map.90 = (bf16[256,1024]{1,0:T(8,128)(2,1)S(1)}, bf16[256,1024]{1,0:T(8,128)(2,1)}) custom-call(bf16[256,512]{1,0:T(8,128)(2,1)S(1)} %collective-permute-done.5.normed_ref, bf16[2,256,512]{2,1,0:T(8,128)(2,1)S(1)} %collective-permute-done.6.near_ref, bf16[3,256,512]{2,1,0:T(8,128)(2,1)S(1)} %copy-done.7, bf16[4,256,512]{2,1,0:T(8,128)(2,1)S(1)} %copy-done.1, ...), custom_call_target="tpu_custom_call" | custom-call | flops 805306368 | bytes 4194304 | tf_op jit(solution)/shard_map/pallas_call | solution.py:180
  69.3 0.0 copy-done.10
  69.4 0.8 copy-done.12
  70.2 2.3 %collective-permute-start.7 = (bf16[256,1024]{1,0:T(8,128)(2,1)}, bf16[256,1024]{1,0:T(8,128)(2,1)}, u32[]{:S(2)}, u32[]{:S(2)}) collective-permute-start(bf16[256,1024]{1,0:T(8,128)(2,1)} %get-tuple-element.24), channel_id=1, source_target_pairs={{0,1},{1,0},{2,3},{3,2},{4,5},{5,4},{6,7},{7,6},{8,9},{9,8},{10,11... | collective-permute-start | bytes 1572872 | tf_op jit(solution)/shard_map/ppermute | solution.py:194
  72.5 0.1 copy.12.rate_ref
  72.6 0.0 collective-permute-done.10.near_ref
  72.7 1.9 %shard_map.91.att_ref = f32[256,512]{1,0:T(8,128)S(1)} custom-call(bf16[2,256,512]{2,1,0:T(8,128)(2,1)} %collective-permute-done.10.near_ref, bf16[3,256,512]{2,1,0:T(8,128)(2,1)S(1)} %copy-done.7, bf16[4,256,512]{2,1,0:T(8,128)(2,1)S(1)} %copy-done.1, bf16[4,256,512]{2,1,0:T(8,128)(2,1)S(1)} %copy-done.3), custom_call_target="tpu_custom_call" | custom-call | flops 268435456 | bytes 4194304 | tf_op jit(solution)/shard_map/pallas_call | solution.py:180
  74.5 3.3 %collective-permute-done.2 = bf16[256,1024]{1,0:T(8,128)(2,1)} collective-permute-done((bf16[256,1024]{1,0:T(8,128)(2,1)}, bf16[256,1024]{1,0:T(8,128)(2,1)}, u32[]{:S(2)}, u32[]{:S(2)}) %collective-permute-start.2) | collective-permute-done | bytes 524320 | tf_op jit(solution)/shard_map/ppermute | solution.py:194
  77.8 1.4 %convert_add_fusion.1 = f32[256,1024]{1,0:T(8,128)S(1)} fusion(bf16[256,1024]{1,0:T(8,128)(2,1)} %collective-permute-done.2, bf16[256,1024]{1,0:T(8,128)(2,1)S(1)} %copy-done.11), kind=kLoop, calls=%fused_computation.1 | loop fusion | flops 786432 | bytes 2097152 | tf_op jit(solution)/shard_map/add | solution.py:195
  79.2 3.3 %collective-permute-start.3 = (bf16[256,512]{1,0:T(8,128)(2,1)S(1)}, bf16[256,512]{1,0:T(8,128)(2,1)S(1)}, u32[]{:S(2)}, u32[]{:S(2)}) collective-permute-start(bf16[256,512]{1,0:T(8,128)(2,1)S(1)} %slice.70), channel_id=1, source_target_pairs={{0,2},{1,3},{2,0},{3,1},{4,6},{5,7},{6,4},{7,5},{8,10},{9,11},{10,... | collective-permute-start | bytes 786440 | tf_op jit(solution)/shard_map/ppermute | solution.py:202
  82.4 12.2 %collective-permute-done.7 = bf16[256,1024]{1,0:T(8,128)(2,1)} collective-permute-done((bf16[256,1024]{1,0:T(8,128)(2,1)}, bf16[256,1024]{1,0:T(8,128)(2,1)}, u32[]{:S(2)}, u32[]{:S(2)}) %collective-permute-start.7) | collective-permute-done | bytes 524320 | tf_op jit(solution)/shard_map/ppermute | solution.py:194
  94.6 1.2 convert_add_fusion
  95.9 2.1 %collective-permute-start.8 = (bf16[256,512]{1,0:T(8,128)(2,1)S(1)}, bf16[256,512]{1,0:T(8,128)(2,1)S(1)}, u32[]{:S(2)}, u32[]{:S(2)}) collective-permute-start(bf16[256,512]{1,0:T(8,128)(2,1)S(1)} %slice.69), channel_id=1, source_target_pairs={{0,2},{1,3},{2,0},{3,1},{4,6},{5,7},{6,4},{7,5},{8,10},{9,11},{10,... | collective-permute-start | bytes 786440 | tf_op jit(solution)/shard_map/ppermute | solution.py:202
  98.0 0.0 collective-permute-done.3
  98.0 0.1 fusion.2
  98.1 0.0 collective-permute-done.9.held_ref
  98.1 4.5 %shard_map.92 = (f32[3,512,512]{2,1,0:T(8,128)S(1)}, bf16[128,1024]{1,0:T(8,128)(2,1)S(1)}, bf16[128,1024]{1,0:T(8,128)(2,1)S(1)}, bf16[128,1024]{1,0:T(8,128)(2,1)S(1)}, bf16[128,1024]{1,0:T(8,128)(2,1)S(1)}) custom-call(bf16[3,512,512]{2,1,0:T(8,128)(2,1)} %collective-permute-done.9.held_ref, bf16[2,256,512]{2,1,0:T(8,128)(2,1)} %collective-permute-done.10.near_ref, ...), custom_call_target="tpu_custom_call" | custom-call | flops 1744830464 | bytes 4194304 | tf_op jit(solution)/shard_map/pallas_call | solution.py:180
  102.6 2.5 %collective-permute-start.11 = (bf16[128,1024]{1,0:T(8,128)(2,1)S(1)}, bf16[128,1024]{1,0:T(8,128)(2,1)S(1)}, u32[]{:S(2)}, u32[]{:S(2)}) collective-permute-start(bf16[128,1024]{1,0:T(8,128)(2,1)S(1)} %get-tuple-element.28), channel_id=1, source_target_pairs={{0,1},{1,0},{2,3},{3,2},{4,5},{5,4},{6,7},{7,6},{8,9},{9,8},{10,11... | collective-permute-start | bytes 786440 | tf_op jit(solution)/shard_map/ppermute | solution.py:194
  105.2 5.7 %collective-permute-done.8 = bf16[256,512]{1,0:T(8,128)(2,1)S(1)} collective-permute-done((bf16[256,512]{1,0:T(8,128)(2,1)S(1)}, bf16[256,512]{1,0:T(8,128)(2,1)S(1)}, u32[]{:S(2)}, u32[]{:S(2)}) %collective-permute-start.8) | collective-permute-done | bytes 262176 | tf_op jit(solution)/shard_map/ppermute | solution.py:202
  110.9 0.1 fusion.3
  111.0 0.1 collective-permute-start.13
  111.1 3.6 %shard_map.93 = f32[1,1,3,512,512]{4,3,2,1,0:T(8,128)} custom-call(f32[3,512,512]{2,1,0:T(8,128)S(1)} %get-tuple-element.31.old_ref, bf16[4,256,512]{2,1,0:T(8,128)(2,1)S(1)} %copy-done.1, bf16[4,256,512]{2,1,0:T(8,128)(2,1)S(1)} %copy-done.3, f32[3,256,1]{2,1,0:T(8,128)S(1)} %copy.11.rate_ref), custom_call_target="tpu_custom_call" | custom-call | flops 805306368 | bytes 4194304 | tf_op jit(solution)/shard_map/pallas_call | solution.py:180
  114.6 1.6 %collective-permute-done.11 = bf16[128,1024]{1,0:T(8,128)(2,1)S(1)} collective-permute-done((bf16[128,1024]{1,0:T(8,128)(2,1)S(1)}, bf16[128,1024]{1,0:T(8,128)(2,1)S(1)}, u32[]{:S(2)}, u32[]{:S(2)}) %collective-permute-start.11) | collective-permute-done | bytes 262176 | tf_op jit(solution)/shard_map/ppermute | solution.py:194
  116.2 0.1 convert_add_fusion.3
  116.3 1.7 %collective-permute-start.12 = (bf16[128,512]{1,0:T(8,128)(2,1)S(1)}, bf16[128,512]{1,0:T(8,128)(2,1)S(1)}, u32[]{:S(2)}, u32[]{:S(2)}) collective-permute-start(bf16[128,512]{1,0:T(8,128)(2,1)S(1)} %slice.72), channel_id=1, source_target_pairs={{0,2},{1,3},{2,0},{3,1},{4,6},{5,7},{6,4},{7,5},{8,10},{9,11},{10,... | collective-permute-start | bytes 393224 | tf_op jit(solution)/shard_map/ppermute | solution.py:202
  118.0 4.6 %collective-permute-done.13 = bf16[128,1024]{1,0:T(8,128)(2,1)S(1)} collective-permute-done((bf16[128,1024]{1,0:T(8,128)(2,1)S(1)}, bf16[128,1024]{1,0:T(8,128)(2,1)S(1)}, u32[]{:S(2)}, u32[]{:S(2)}) %collective-permute-start.13) | collective-permute-done | bytes 262176 | tf_op jit(solution)/shard_map/ppermute | solution.py:194
  122.6 0.1 convert_add_fusion.2
  122.7 0.5 collective-permute-start.14
  123.2 1.3 collective-permute-done.12
  124.5 6.2 %collective-permute-done.14 = bf16[128,512]{1,0:T(8,128)(2,1)S(1)} collective-permute-done((bf16[128,512]{1,0:T(8,128)(2,1)S(1)}, bf16[128,512]{1,0:T(8,128)(2,1)S(1)}, u32[]{:S(2)}, u32[]{:S(2)}) %collective-permute-start.14) | collective-permute-done | bytes 131104 | tf_op jit(solution)/shard_map/ppermute | solution.py:202
  130.8 1.0 pad_maximum_fusion
  (27 shorter events, 0.2 us)
Async XLA Ops:
  0.6 1.2 copy-start
  1.9 1.2 copy-start.2
  3.1 1.1 copy-start.6
  4.2 5.3 %copy-start.17 = (f32[3,256,1]{1,2,0:T(1,128)S(1)}, f32[3,256,1]{1,2,0:T(1,128)}, u32[]{:S(2)}) copy-start(f32[3,256,1]{1,2,0:T(1,128)} %param.10) | copy-start | bytes 9220
  4.2 5.5 %copy-start.1 = (bf16[4,256,512]{2,1,0:T(8,128)(2,1)S(1)}, bf16[4,256,512]{2,1,0:T(8,128)(2,1)}, u32[]{:S(2)}) copy-start(bf16[4,256,512]{2,1,0:T(8,128)(2,1)} %key_ref.3) | copy-start | bytes 3145732
  4.2 5.5 %copy-start.3 = (bf16[4,256,512]{2,1,0:T(8,128)(2,1)S(1)}, bf16[4,256,512]{2,1,0:T(8,128)(2,1)}, u32[]{:S(2)}) copy-start(bf16[4,256,512]{2,1,0:T(8,128)(2,1)} %val_ref.3) | copy-start | bytes 3145732
  5.4 0.8 copy-start.15
  6.2 52.6 %collective-permute-start = (bf16[2,256,512]{2,1,0:T(8,128)(2,1)}, bf16[2,256,512]{2,1,0:T(8,128)(2,1)}, u32[]{:S(2)}, u32[]{:S(2)}) collective-permute-start(bf16[2,256,512]{2,1,0:T(8,128)(2,1)} %get-tuple-element.17), channel_id=1, source_target_pairs={{0,4},{4,8},{8,12},{12,16},{16,20},{20,24},{24,28},{28,0},{1,5},{5... | collective-permute-start | bytes 1572872 | tf_op jit(solution)/shard_map/ppermute | solution.py:16
  6.7 11.8 %collective-permute-start.4 = (bf16[256,512]{1,0:T(8,128)(2,1)}, bf16[256,512]{1,0:T(8,128)(2,1)S(1)}, u32[]{:S(2)}, u32[]{:S(2)}) collective-permute-start(bf16[256,512]{1,0:T(8,128)(2,1)} %get-tuple-element.21), channel_id=1, source_target_pairs={{0,28},{4,0},{8,4},{12,8},{16,12},{20,16},{24,20},{28,24},{1,29},{... | collective-permute-start | bytes 786440 | tf_op jit(solution)/shard_map/ppermute | solution.py:16
  9.7 1.9 %copy-start.4 = (f32[1,1,3,512,512]{4,3,2,1,0:T(8,128)S(1)}, f32[1,1,3,512,512]{4,3,2,1,0:T(8,128)}, u32[]{:S(2)}) copy-start(f32[1,1,3,512,512]{4,3,2,1,0:T(8,128)} %old_ref.3) | copy-start | bytes 9437188
  11.6 4.3 %copy-start.16 = (bf16[2,256,512]{2,1,0:T(8,128)(2,1)S(1)}, bf16[2,256,512]{2,1,0:T(8,128)(2,1)}, u32[]{:S(2)}) copy-start(bf16[2,256,512]{2,1,0:T(8,128)(2,1)} %copy-done.15) | copy-start | bytes 1572868
  11.6 6.9 %copy-start.14 = (f32[512]{0:T(512)S(1)}, f32[512]{0:T(512)}, u32[]{:S(2)}) copy-start(f32[512]{0:T(512)} %param.11) | copy-start | bytes 6148
  11.6 47.2 %copy-start.5 = (f32[1,1,3,512,512]{4,3,2,1,0:T(8,128)S(1)}, f32[1,1,3,512,512]{4,3,2,1,0:T(8,128)}, u32[]{:S(2)}) copy-start(f32[1,1,3,512,512]{4,3,2,1,0:T(8,128)} %old_ref.3) | copy-start | bytes 9437188
  11.6 47.2 %copy-start.7 = (bf16[3,256,512]{2,1,0:T(8,128)(2,1)S(1)}, bf16[3,256,512]{2,1,0:T(8,128)(2,1)}, u32[]{:S(2)}) copy-start(bf16[3,256,512]{2,1,0:T(8,128)(2,1)} %q_ref.9) | copy-start | bytes 2359300
  11.6 47.2 %copy-start.8 = (bf16[512,2048]{1,0:T(8,128)(2,1)S(1)}, bf16[512,2048]{1,0:T(8,128)(2,1)}, u32[]{:S(2)}) copy-start(bf16[512,2048]{1,0:T(8,128)(2,1)} %w_ref.5) | copy-start | bytes 6291460
  14.6 83.5 %collective-permute-start.9 = (bf16[3,512,512]{2,1,0:T(8,128)(2,1)}, bf16[3,512,512]{2,1,0:T(8,128)(2,1)}, u32[]{:S(2)}, u32[]{:S(2)}) collective-permute-start(bf16[3,512,512]{2,1,0:T(8,128)(2,1)} %shard_map.88.held_ref), channel_id=1, source_target_pairs={{0,8},{4,12},{8,16},{12,20},{16,24},{20,28},{24,0},{28,4},{1,9},{5... | collective-permute-start | bytes 4718600 | tf_op jit(solution)/shard_map/ppermute | solution.py:16
  15.9 51.2 %collective-permute-start.6 = (bf16[2,256,512]{2,1,0:T(8,128)(2,1)S(1)}, bf16[2,256,512]{2,1,0:T(8,128)(2,1)S(1)}, u32[]{:S(2)}, u32[]{:S(2)}) collective-permute-start(bf16[2,256,512]{2,1,0:T(8,128)(2,1)S(1)} %copy-done.16), channel_id=1, source_target_pairs={{0,4},{4,8},{8,12},{12,16},{16,20},{20,24},{24,28},{28,0},{1,5},{5... | collective-permute-start | bytes 1572872 | tf_op jit(solution)/shard_map/ppermute | solution.py:16
  15.9 42.8 %collective-permute-start.1 = (f32[1,256]{1,0:T(1,128)S(1)}, f32[1,256]{1,0:T(1,128)S(1)}, u32[]{:S(2)}, u32[]{:S(2)}) collective-permute-start(f32[1,256]{1,0:T(1,128)S(1)} %slice_bitcast_fusion), channel_id=1, source_target_pairs={{0,4},{4,8},{8,12},{12,16},{16,20},{20,24},{24,28},{28,0},{1,5},{5... | collective-permute-start | bytes 3080 | tf_op jit(solution)/shard_map/ppermute | solution.py:16
  18.5 54.2 %collective-permute-start.10 = (bf16[2,256,512]{2,1,0:T(8,128)(2,1)}, bf16[2,256,512]{2,1,0:T(8,128)(2,1)}, u32[]{:S(2)}, u32[]{:S(2)}) collective-permute-start(bf16[2,256,512]{2,1,0:T(8,128)(2,1)} %get-tuple-element.25), channel_id=1, source_target_pairs={{0,4},{4,8},{8,12},{12,16},{16,20},{20,24},{24,28},{28,0},{1,5},{5... | collective-permute-start | bytes 1572872 | tf_op jit(solution)/shard_map/ppermute | solution.py:16
  58.8 8.4 %collective-permute-start.5 = (bf16[256,512]{1,0:T(8,128)(2,1)S(1)}, bf16[256,512]{1,0:T(8,128)(2,1)S(1)}, u32[]{:S(2)}, u32[]{:S(2)}) collective-permute-start(bf16[256,512]{1,0:T(8,128)(2,1)S(1)} %shard_map.89), channel_id=1, source_target_pairs={{0,4},{4,8},{8,12},{12,16},{16,20},{20,24},{24,28},{28,0},{1,5},{5... | collective-permute-start | bytes 786440 | tf_op jit(solution)/shard_map/ppermute | solution.py:16
  62.5 6.8 %copy-start.10 = (bf16[256,1024]{1,0:T(8,128)(2,1)}, bf16[256,1024]{1,0:T(8,128)(2,1)S(1)}, u32[]{:S(2)}) copy-start(bf16[256,1024]{1,0:T(8,128)(2,1)S(1)} %get-tuple-element.19) | copy-start | bytes 1572868
  62.5 15.3 %collective-permute-start.2 = (bf16[256,1024]{1,0:T(8,128)(2,1)}, bf16[256,1024]{1,0:T(8,128)(2,1)}, u32[]{:S(2)}, u32[]{:S(2)}) collective-permute-start(bf16[256,1024]{1,0:T(8,128)(2,1)} %get-tuple-element.20), channel_id=1, source_target_pairs={{0,1},{1,0},{2,3},{3,2},{4,5},{5,4},{6,7},{7,6},{8,9},{9,8},{10,11... | collective-permute-start | bytes 1572872 | tf_op jit(solution)/shard_map/ppermute | solution.py:194
  69.3 0.8 copy-start.12
  70.2 24.4 %collective-permute-start.7 = (bf16[256,1024]{1,0:T(8,128)(2,1)}, bf16[256,1024]{1,0:T(8,128)(2,1)}, u32[]{:S(2)}, u32[]{:S(2)}) collective-permute-start(bf16[256,1024]{1,0:T(8,128)(2,1)} %get-tuple-element.24), channel_id=1, source_target_pairs={{0,1},{1,0},{2,3},{3,2},{4,5},{5,4},{6,7},{7,6},{8,9},{9,8},{10,11... | collective-permute-start | bytes 1572872 | tf_op jit(solution)/shard_map/ppermute | solution.py:194
  72.6 5.2 %copy-start.11 = (bf16[256,1024]{1,0:T(8,128)(2,1)S(1)}, bf16[256,1024]{1,0:T(8,128)(2,1)}, u32[]{:S(2)}) copy-start(bf16[256,1024]{1,0:T(8,128)(2,1)} %copy-done.10) | copy-start | bytes 1572868
  72.6 22.0 %copy-start.13 = (bf16[256,1024]{1,0:T(8,128)(2,1)S(1)}, bf16[256,1024]{1,0:T(8,128)(2,1)}, u32[]{:S(2)}) copy-start(bf16[256,1024]{1,0:T(8,128)(2,1)} %copy-done.12) | copy-start | bytes 1572868
  77.8 20.3 %copy-start.9 = (bf16[512,2048]{1,0:T(8,128)(2,1)S(1)}, bf16[512,2048]{1,0:T(8,128)(2,1)}, u32[]{:S(2)}) copy-start(bf16[512,2048]{1,0:T(8,128)(2,1)} %w_ref.5) | copy-start | bytes 6291460
  79.2 18.8 %collective-permute-start.3 = (bf16[256,512]{1,0:T(8,128)(2,1)S(1)}, bf16[256,512]{1,0:T(8,128)(2,1)S(1)}, u32[]{:S(2)}, u32[]{:S(2)}) collective-permute-start(bf16[256,512]{1,0:T(8,128)(2,1)S(1)} %slice.70), channel_id=1, source_target_pairs={{0,2},{1,3},{2,0},{3,1},{4,6},{5,7},{6,4},{7,5},{8,10},{9,11},{10,... | collective-permute-start | bytes 786440 | tf_op jit(solution)/shard_map/ppermute | solution.py:202
  95.9 15.0 %collective-permute-start.8 = (bf16[256,512]{1,0:T(8,128)(2,1)S(1)}, bf16[256,512]{1,0:T(8,128)(2,1)S(1)}, u32[]{:S(2)}, u32[]{:S(2)}) collective-permute-start(bf16[256,512]{1,0:T(8,128)(2,1)S(1)} %slice.69), channel_id=1, source_target_pairs={{0,2},{1,3},{2,0},{3,1},{4,6},{5,7},{6,4},{7,5},{8,10},{9,11},{10,... | collective-permute-start | bytes 786440 | tf_op jit(solution)/shard_map/ppermute | solution.py:202
  102.6 13.6 %collective-permute-start.11 = (bf16[128,1024]{1,0:T(8,128)(2,1)S(1)}, bf16[128,1024]{1,0:T(8,128)(2,1)S(1)}, u32[]{:S(2)}, u32[]{:S(2)}) collective-permute-start(bf16[128,1024]{1,0:T(8,128)(2,1)S(1)} %get-tuple-element.28), channel_id=1, source_target_pairs={{0,1},{1,0},{2,3},{3,2},{4,5},{5,4},{6,7},{7,6},{8,9},{9,8},{10,11... | collective-permute-start | bytes 786440 | tf_op jit(solution)/shard_map/ppermute | solution.py:194
  111.0 11.7 %collective-permute-start.13 = (bf16[128,1024]{1,0:T(8,128)(2,1)S(1)}, bf16[128,1024]{1,0:T(8,128)(2,1)S(1)}, u32[]{:S(2)}, u32[]{:S(2)}) collective-permute-start(bf16[128,1024]{1,0:T(8,128)(2,1)S(1)} %get-tuple-element.30), channel_id=1, source_target_pairs={{0,1},{1,0},{2,3},{3,2},{4,5},{5,4},{6,7},{7,6},{8,9},{9,8},{10,11... | collective-permute-start | bytes 786440 | tf_op jit(solution)/shard_map/ppermute | solution.py:194
  116.3 8.2 %collective-permute-start.12 = (bf16[128,512]{1,0:T(8,128)(2,1)S(1)}, bf16[128,512]{1,0:T(8,128)(2,1)S(1)}, u32[]{:S(2)}, u32[]{:S(2)}) collective-permute-start(bf16[128,512]{1,0:T(8,128)(2,1)S(1)} %slice.72), channel_id=1, source_target_pairs={{0,2},{1,3},{2,0},{3,1},{4,6},{5,7},{6,4},{7,5},{8,10},{9,11},{10,... | collective-permute-start | bytes 393224 | tf_op jit(solution)/shard_map/ppermute | solution.py:202
  122.7 8.0 %collective-permute-start.14 = (bf16[128,512]{1,0:T(8,128)(2,1)S(1)}, bf16[128,512]{1,0:T(8,128)(2,1)S(1)}, u32[]{:S(2)}, u32[]{:S(2)}) collective-permute-start(bf16[128,512]{1,0:T(8,128)(2,1)S(1)} %slice.71), channel_id=1, source_target_pairs={{0,2},{1,3},{2,0},{3,1},{4,6},{5,7},{6,4},{7,5},{8,10},{9,11},{10,... | collective-permute-start | bytes 393224 | tf_op jit(solution)/shard_map/ppermute | solution.py:202
where the time goes:
time: 132 us
  waiting for transfers between devices  75.3 us (57%)
  starting transfers between devices  22.1 us (17%)
  Pallas kernels  22 us (17%)
  local copies, waits for them, and re-layouts  7.54 us (6%)
  other arithmetic  3.91 us (3%)
    ppermute x7, waiting for transfers between devices, shifted(): return lax.ppermute(x, axis, [(i, (i + by) % count) for i in range(count)])  40.4 us
    pallas_call x8, Pallas kernels, call(): pl.pallas_call(kernel, out_shape=shapes, grid=(1,), in_specs=specs, out_s...  22 us
    ppermute x4, waiting for transfers between devices, pair_sum(): got = lax.ppermute(send, 'head', [(i, i ^ 1) for i in range(count)])  21.6 us
    ppermute x4, waiting for transfers between devices, last_sum(): got = lax.ppermute(far, 'head', [(i, i ^ 2) for i in range(count)])  13.2 us
    ppermute x4, starting transfers between devices, last_sum(): got = lax.ppermute(far, 'head', [(i, i ^ 2) for i in range(count)])  7.52 us
    unnamed x37, local copies, waits for them, and re-layouts  7.3 us
    ppermute x7, starting transfers between devices, shifted(): return lax.ppermute(x, axis, [(i, (i + by) % count) for i in range(count)])  7.29 us
    ppermute x4, starting transfers between devices, pair_sum(): got = lax.ppermute(send, 'head', [(i, i ^ 1) for i in range(count)])  7.25 us
  transfers between devices with their start and end apart: 15, of which 9 were waited for; matrix products, arithmetic and copies ran while one was open for 3% of the time, Pallas kernels for 16%

commit v1 on v0

--- a/solution.py
+++ b/solution.py
@@ -85,9 +85,14 @@
         out[:, slot * width : (slot + 1) * width] = piece
 
 
-def split_kernel(q_ref, key0, key1, key2, val0, val1, val2, q_out, near0, near1, near2):
+def split_first_kernel(q_ref, key0, val0, q_out, near0):
     q_out[...] = q_ref[0]
-    for out, k_ref, v_ref in ((near0, key0, val0), (near1, key1, val1), (near2, key2, val2)):
+    near0[0] = key0[0]
+    near0[1] = val0[0]
+
+
+def split_kernel(key1, key2, val1, val2, near1, near2):
+    for out, k_ref, v_ref in ((near1, key1, val1), (near2, key2, val2)):
         out[0] = k_ref[0]
         out[1] = v_ref[0]
 
@@ -146,10 +151,11 @@
     rounded = [state_ref[i].astype(BF16) for i in range(3)]
     normed = normed_apply(rounded, q_ref[0], gain_ref[...])
     combined = (att_ref[...] + normed).astype(BF16)
-    rows = halves[0].shape[0]
-    for at_row in range(0, combined.shape[0], rows):
-        keep, send = halves[2 * (at_row // rows) :][:2]
+    at_row = 0
+    for keep, send in zip(halves[::2], halves[1::2]):
+        rows = keep.shape[0]
         project(combined[at_row : at_row + rows], w_ref, keep, send)
+        at_row += rows
 
 
 def last_kernel(old_ref, key_ref, val_ref, rate_ref, out_ref):
@@ -173,7 +179,7 @@
     return pl.BlockSpec((1,) + x.shape[1:], lambda i: (index,) + (0,) * (len(x.shape) - 1))
 
 
-def call(kernel, args, outs, flops):
+def call(kernel, args, outs, flops, vmem=40 << 20):
     arrays = [a[0] if isinstance(a, tuple) else a for a in args]
     specs = [at(*a) if isinstance(a, tuple) else whole(a) for a in args]
     shapes = [jax.ShapeDtypeStruct(s, t) for s, t in outs]
@@ -183,7 +189,7 @@
         grid=(1,),
         in_specs=specs,
         out_specs=[whole(s) for s in shapes],
-        compiler_params=pltpu.CompilerParams(vmem_limit_bytes=40 << 20),
+        compiler_params=pltpu.CompilerParams(vmem_limit_bytes=vmem),
         cost_estimate=pl.CostEstimate(flops=flops, bytes_accessed=4 << 20, transcendentals=0),
     )(*arrays)
     return got
@@ -209,16 +215,21 @@
     unit = 2 * rows * size * size
     gain_row = norm_gain[None, :]
     wide = out_weight.shape[1] // 2
-    half, quarter = ((rows, wide), BF16), ((rows // 2, wide), BF16)
+    half = ((rows, wide), BF16)
+    chunks = (3 * rows // 8, 3 * rows // 8, rows // 4)
     both = ((2, rows, size), BF16)
     block = ((rows, size), BF16)
 
     rate_near = shifted(learn_rates[1].reshape(1, -1), "seq", 1).reshape(-1, 1)
-    ahead, near0, near1, near2 = call(
+    ahead, near0 = call(
+        split_first_kernel, [(queries, 1), (key_vectors, 0), (values, 0)], [block, both], 0, 60 << 20
+    )
+    near1, near2 = call(
         split_kernel,
-        [(queries, 1)] + [(key_vectors, t) for t in range(3)] + [(values, t) for t in range(3)],
-        [block, both, both, both],
+        [(key_vectors, 1), (key_vectors, 2), (values, 1), (values, 2)],
+        [both, both],
         0,
+        60 << 20,
     )
     ahead = shifted(ahead, "seq", -1)
     near0 = shifted(near0, "seq", 1)
@@ -240,7 +251,7 @@
     near0, rate_near = lax.optimization_barrier((near0, rate_near))
     sums = [
         pair_sum(
-            *call(mix_first_kernel, [incoming, near0, *window(0), gain_row, out_weight], [half] * 2, 9 * unit)
+            *call(mix_first_kernel, [incoming, near0, *window(0), gain_row, out_weight], [half] * 2, 9 * unit),
         )
     ]
     sums.append(pair_sum(*call(mix_kernel, [normed, near1, *window(1), out_weight], [half] * 2, 6 * unit)))
@@ -248,17 +259,27 @@
     state, *halves = call(
         middle_kernel,
         [held, near2, rate_near, (queries, 2), gain_row, att, out_weight],
-        [((3, size, size), F32)] + [quarter] * 4,
+        [((3, size, size), F32)] + [((c, wide), BF16) for c in chunks for _ in range(2)],
         13 * unit,
     )
-    outputs = [last_sum(*pair) for pair in sums]
-    lower = last_sum(*pair_sum(*halves[:2]))
-    upper = last_sum(*pair_sum(*halves[2:]))
-    outputs.append(jnp.concatenate([lower, upper], axis=0))
     (outgoing,) = call(
-        last_kernel, [state, (key_vectors, 3), (values, 3), (learn_rates, 2)], [(incoming.shape, F32)], 6 * unit
-    )
-    return (jnp.stack(outputs), outgoing)
+        last_kernel,
+        [state, (key_vectors, 3), (values, 3), (learn_rates, 2)],
+        [(incoming.shape, F32)],
+        6 * unit,
+    )
+    own, outgoing = lax.optimization_barrier((sums[1][0], outgoing))
+    sums[1] = (own, sums[1][1])
+    pieces = [(t, 0, last_sum(*pair)) for t, pair in enumerate(sums)]
+    at_row = 0
+    for i, chunk in enumerate(chunks):
+        pair = pair_sum(*halves[2 * i : 2 * i + 2])
+        pieces.append((last, at_row, last_sum(*pair)))
+        at_row += chunk
+    out = jnp.zeros(queries.shape, BF16)
+    for t, row, piece in pieces:
+        out = lax.dynamic_update_slice(out, piece[None], (t, row, 0))
+    return (out, outgoing)
 
 
 def solution(mesh):

time: 132 us -> 130 us (0.985)
  waiting for transfers between devices: 75.3 us -> 70.2 us
  Pallas kernels: 22 us -> 26.7 us
  local copies, waits for them, and re-layouts: 7.54 us -> 4.9 us
  starting transfers between devices: 22.1 us -> 24.3 us
    ppermute x4 -> x5, waiting for transfers between devices: 13.2 us -> 6.83 us  [last_sum(): got = lax.ppermute(far, 'head', [(i, i ^ 2) for i in range(count)])]
    pallas_call x8 -> x9, Pallas kernels: 22 us -> 26.7 us  [call(): pl.pallas_call(kernel, out_shape=shapes, grid=(1,), in_specs=specs, out_s...]
    ppermute x4 -> x5, waiting for transfers between devices: 21.6 us -> 25.9 us  [pair_sum(): got = lax.ppermute(send, 'head', [(i, i ^ 1) for i in range(count)])]
    ppermute x7, waiting for transfers between devices: 40.4 us -> 37.5 us  [shifted(): return lax.ppermute(x, axis, [(i, (i + by) % count) for i in range(count)])]
    unnamed x37 -> x31, local copies, waits for them, and re-layouts: 7.3 us -> 4.6 us
    ppermute x4 -> x5, starting transfers between devices: 7.25 us -> 9.21 us  [pair_sum(): got = lax.ppermute(send, 'head', [(i, i ^ 1) for i in range(count)])]
    ppermute x4 -> x5, starting transfers between devices: 7.52 us -> 7.84 us  [last_sum(): got = lax.ppermute(far, 'head', [(i, i ^ 2) for i in range(count)])]
    add x4 -> x5, other arithmetic: 2.7 us -> 2.55 us  [pair_sum(): pair = keep.astype(F32) + got.astype(F32)]
  transfers between devices with their start and end apart: 15 -> 17, of which waited for: 9 -> 9; matrix products, arithmetic and copies ran while one was open for 3% -> 2% of each run, Pallas kernels for 16% -> 19%
where the time goes in v1:
time: 130 us
  waiting for transfers between devices  70.2 us (54%)
  Pallas kernels  26.7 us (21%)
  starting transfers between devices  24.3 us (19%)
  local copies, waits for them, and re-layouts  4.9 us (4%)
  other arithmetic  2.76 us (2%)
    ppermute x7, waiting for transfers between devices, shifted(): return lax.ppermute(x, axis, [(i, (i + by) % count) for i in range(count)])  37.5 us
    pallas_call x9, Pallas kernels, call(): pl.pallas_call(kernel, out_shape=shapes, grid=(1,), in_specs=specs, out_s...  26.7 us
    ppermute x5, waiting for transfers between devices, pair_sum(): got = lax.ppermute(send, 'head', [(i, i ^ 1) for i in range(count)])  25.9 us
    ppermute x5, starting transfers between devices, pair_sum(): got = lax.ppermute(send, 'head', [(i, i ^ 1) for i in range(count)])  9.21 us
    ppermute x5, starting transfers between devices, last_sum(): got = lax.ppermute(far, 'head', [(i, i ^ 2) for i in range(count)])  7.84 us
    ppermute x7, starting transfers between devices, shifted(): return lax.ppermute(x, axis, [(i, (i + by) % count) for i in range(count)])  7.21 us
    ppermute x5, waiting for transfers between devices, last_sum(): got = lax.ppermute(far, 'head', [(i, i ^ 2) for i in range(count)])  6.83 us
    unnamed x31, local copies, waits for them, and re-layouts  4.6 us
  transfers between devices with their start and end apart: 17, of which 9 were waited for; matrix products, arithmetic and copies ran while one was open for 2% of the time, Pallas kernels for 19%

profile of v1, /device:TPU:0, one launch (start us, length us, event | category | flops | bytes accessed | tf_op | source)
XLA Modules:
  0.0 129.8 jit_solution(12308949215238625953)
XLA Ops:
  0.6 0.0 copy-start.1
  0.6 0.0 copy-start
  0.7 0.0 copy-start.14
  0.7 2.2 %shard_map.86 = (bf16[256,512]{1,0:T(8,128)(2,1)}, bf16[2,256,512]{2,1,0:T(8,128)(2,1)}) custom-call(bf16[3,256,512]{2,1,0:T(8,128)(2,1)} %q_ref.9, bf16[4,256,512]{2,1,0:T(8,128)(2,1)} %key_ref.3, bf16[4,256,512]{2,1,0:T(8,128)(2,1)} %val_ref.3), custom_call_target="tpu_custom_call" | custom-call | bytes 4194304 | tf_op jit(solution)/shard_map/pallas_call | solution.py:186
  2.8 0.5 collective-permute-start
  3.3 2.9 %collective-permute-start.4 = (bf16[256,512]{1,0:T(8,128)(2,1)}, bf16[256,512]{1,0:T(8,128)(2,1)S(1)}, u32[]{:S(2)}, u32[]{:S(2)}) collective-permute-start(bf16[256,512]{1,0:T(8,128)(2,1)} %get-tuple-element.25), channel_id=1, source_target_pairs={{0,28},{4,0},{8,4},{12,8},{16,12},{20,16},{24,20},{28,24},{1,29},{... | collective-permute-start | bytes 786440 | tf_op jit(solution)/shard_map/ppermute | solution.py:16
  6.2 2.2 %shard_map.90 = (bf16[2,256,512]{2,1,0:T(8,128)(2,1)}, bf16[2,256,512]{2,1,0:T(8,128)(2,1)}) custom-call(bf16[4,256,512]{2,1,0:T(8,128)(2,1)} %key_ref.3, bf16[4,256,512]{2,1,0:T(8,128)(2,1)} %key_ref.3, bf16[4,256,512]{2,1,0:T(8,128)(2,1)} %val_ref.3, bf16[4,256,512]{2,1,0:T(8,128)(2,1)} %val_ref.3), custom_call_target="tpu_custom_call" | custom-call | bytes 4194304 | tf_op jit(solution)/shard_map/pallas_call | solution.py:186
  8.4 0.0 collective-permute-start.6
  8.4 0.2 copy.11.rate_ref
  8.6 0.0 copy-start.2
  8.6 1.9 %copy-done.2 = f32[1,1,3,512,512]{4,3,2,1,0:T(8,128)S(1)} copy-done((f32[1,1,3,512,512]{4,3,2,1,0:T(8,128)S(1)}, f32[1,1,3,512,512]{4,3,2,1,0:T(8,128)}, u32[]{:S(2)}) %copy-start.2) | copy-done | bytes 3145752
  10.5 2.9 %shard_map.88.held_ref = bf16[3,512,512]{2,1,0:T(8,128)(2,1)} custom-call(f32[1,1,3,512,512]{4,3,2,1,0:T(8,128)S(1)} %copy-done.2, bf16[4,256,512]{2,1,0:T(8,128)(2,1)S(1)} %copy-done, bf16[4,256,512]{2,1,0:T(8,128)(2,1)S(1)} %copy-done.1, f32[3,256,1]{2,1,0:T(8,128)S(1)} %copy.11.rate_ref), custom_call_target="tpu_custom_call" | custom-call | flops 805306368 | bytes 4194304 | tf_op jit(solution)/shard_map/pallas_call | solution.py:186
  13.5 1.3 %collective-permute-start.8 = (bf16[3,512,512]{2,1,0:T(8,128)(2,1)}, bf16[3,512,512]{2,1,0:T(8,128)(2,1)}, u32[]{:S(2)}, u32[]{:S(2)}) collective-permute-start(bf16[3,512,512]{2,1,0:T(8,128)(2,1)} %shard_map.88.held_ref), channel_id=1, source_target_pairs={{0,8},{4,12},{8,16},{12,20},{16,24},{20,28},{24,0},{28,4},{1,9},{5... | collective-permute-start | bytes 4718600 | tf_op jit(solution)/shard_map/ppermute | solution.py:16
  14.8 2.2 %collective-permute-start.1 = (f32[1,256]{1,0:T(1,128)S(1)}, f32[1,256]{1,0:T(1,128)S(1)}, u32[]{:S(2)}, u32[]{:S(2)}) collective-permute-start(f32[1,256]{1,0:T(1,128)S(1)} %slice_bitcast_fusion), channel_id=1, source_target_pairs={{0,4},{4,8},{8,12},{12,16},{16,20},{20,24},{24,28},{28,0},{1,5},{5... | collective-permute-start | bytes 3080 | tf_op jit(solution)/shard_map/ppermute | solution.py:16
  17.0 0.0 collective-permute-done.4.q_ref
  17.0 0.3 collective-permute-start.9
  17.3 2.1 %shard_map.89 = bf16[256,512]{1,0:T(8,128)(2,1)S(1)} custom-call(bf16[3,512,512]{2,1,0:T(8,128)(2,1)} %shard_map.88.held_ref, bf16[256,512]{1,0:T(8,128)(2,1)S(1)} %collective-permute-done.4.q_ref, f32[1,512]{1,0:T(1,128)S(1)} %bitcast.22), custom_call_target="tpu_custom_call" | custom-call | flops 402653184 | bytes 4194304 | tf_op jit(solution)/shard_map/pallas_call | solution.py:186
  19.5 35.9 %collective-permute-done.1 = f32[1,256]{1,0:T(1,128)S(1)} collective-permute-done((f32[1,256]{1,0:T(1,128)S(1)}, f32[1,256]{1,0:T(1,128)S(1)}, u32[]{:S(2)}, u32[]{:S(2)}) %collective-permute-start.1) | collective-permute-done | bytes 1056 | tf_op jit(solution)/shard_map/ppermute | solution.py:16
  55.4 0.0 collective-permute-start.5
  55.4 0.0 collective-permute-done.near_ref
  55.4 3.7 %shard_map.87 = (bf16[256,1024]{1,0:T(8,128)(2,1)S(1)}, bf16[256,1024]{1,0:T(8,128)(2,1)}) custom-call(f32[1,1,3,512,512]{4,3,2,1,0:T(8,128)S(1)} %copy-done.3, bf16[2,256,512]{2,1,0:T(8,128)(2,1)} %collective-permute-done.near_ref, bf16[3,256,512]{2,1,0:T(8,128)(2,1)S(1)} %copy-done.4, bf16[4,256,512]{2,1,0:T(8,128)(2,1)S(1)} %copy-done, ...), custom_call_target="tpu_custom_call" | custom-call | flops 1207959552 | bytes 4194304 | tf_op jit(solution)/shard_map/pallas_call | solution.py:186
  59.1 0.8 copy-done.7
  59.9 2.3 %collective-permute-start.2 = (bf16[256,1024]{1,0:T(8,128)(2,1)}, bf16[256,1024]{1,0:T(8,128)(2,1)}, u32[]{:S(2)}, u32[]{:S(2)}) collective-permute-start(bf16[256,1024]{1,0:T(8,128)(2,1)} %get-tuple-element.24), channel_id=1, source_target_pairs={{0,1},{1,0},{2,3},{3,2},{4,5},{5,4},{6,7},{7,6},{8,9},{9,8},{10,11... | collective-permute-start | bytes 1572872 | tf_op jit(solution)/shard_map/ppermute | solution.py:200
  62.3 0.0 collective-permute-done.6.near_ref
  62.3 1.6 %collective-permute-done.5.normed_ref = bf16[256,512]{1,0:T(8,128)(2,1)S(1)} collective-permute-done((bf16[256,512]{1,0:T(8,128)(2,1)S(1)}, bf16[256,512]{1,0:T(8,128)(2,1)S(1)}, u32[]{:S(2)}, u32[]{:S(2)}) %collective-permute-start.5) | collective-permute-done | bytes 262176 | tf_op jit(solution)/shard_map/ppermute | solution.py:16
  63.8 3.2 %shard_map.91 = (bf16[256,1024]{1,0:T(8,128)(2,1)S(1)}, bf16[256,1024]{1,0:T(8,128)(2,1)}) custom-call(bf16[256,512]{1,0:T(8,128)(2,1)S(1)} %collective-permute-done.5.normed_ref, bf16[2,256,512]{2,1,0:T(8,128)(2,1)} %collective-permute-done.6.near_ref, bf16[3,256,512]{2,1,0:T(8,128)(2,1)S(1)} %copy-done.4, bf16[4,256,512]{2,1,0:T(8,128)(2,1)S(1)} %copy-done, ...), custom_call_target="tpu_custom_call" | custom-call | flops 805306368 | bytes 4194304 | tf_op jit(solution)/shard_map/pallas_call | solution.py:186
  67.1 0.8 copy-done.9
  67.9 2.3 %collective-permute-start.7 = (bf16[256,1024]{1,0:T(8,128)(2,1)}, bf16[256,1024]{1,0:T(8,128)(2,1)}, u32[]{:S(2)}, u32[]{:S(2)}) collective-permute-start(bf16[256,1024]{1,0:T(8,128)(2,1)} %get-tuple-element.28), channel_id=1, source_target_pairs={{0,1},{1,0},{2,3},{3,2},{4,5},{5,4},{6,7},{7,6},{8,9},{9,8},{10,11... | collective-permute-start | bytes 1572872 | tf_op jit(solution)/shard_map/ppermute | solution.py:200
  70.2 0.1 copy.12.rate_ref
  70.3 0.0 collective-permute-done.9.near_ref
  70.4 1.9 %shard_map.92.att_ref = f32[256,512]{1,0:T(8,128)S(1)} custom-call(bf16[2,256,512]{2,1,0:T(8,128)(2,1)} %collective-permute-done.9.near_ref, bf16[3,256,512]{2,1,0:T(8,128)(2,1)S(1)} %copy-done.4, bf16[4,256,512]{2,1,0:T(8,128)(2,1)S(1)} %copy-done, bf16[4,256,512]{2,1,0:T(8,128)(2,1)S(1)} %copy-done.1), custom_call_target="tpu_custom_call" | custom-call | flops 268435456 | bytes 4194304 | tf_op jit(solution)/shard_map/pallas_call | solution.py:186
  72.2 3.0 %collective-permute-done.2 = bf16[256,1024]{1,0:T(8,128)(2,1)} collective-permute-done((bf16[256,1024]{1,0:T(8,128)(2,1)}, bf16[256,1024]{1,0:T(8,128)(2,1)}, u32[]{:S(2)}, u32[]{:S(2)}) %collective-permute-start.2) | collective-permute-done | bytes 524320 | tf_op jit(solution)/shard_map/ppermute | solution.py:200
  75.2 1.2 convert_add_fusion.1
  76.4 0.0 copy-start.6
  76.5 3.3 %collective-permute-start.3 = (bf16[256,512]{1,0:T(8,128)(2,1)S(1)}, bf16[256,512]{1,0:T(8,128)(2,1)S(1)}, u32[]{:S(2)}, u32[]{:S(2)}) collective-permute-start(bf16[256,512]{1,0:T(8,128)(2,1)S(1)} %slice.92), channel_id=1, source_target_pairs={{0,2},{1,3},{2,0},{3,1},{4,6},{5,7},{6,4},{7,5},{8,10},{9,11},{10,... | collective-permute-start | bytes 786440 | tf_op jit(solution)/shard_map/ppermute | solution.py:208
  79.7 12.3 %collective-permute-done.7 = bf16[256,1024]{1,0:T(8,128)(2,1)} collective-permute-done((bf16[256,1024]{1,0:T(8,128)(2,1)}, bf16[256,1024]{1,0:T(8,128)(2,1)}, u32[]{:S(2)}, u32[]{:S(2)}) %collective-permute-start.7) | collective-permute-done | bytes 524320 | tf_op jit(solution)/shard_map/ppermute | solution.py:200
  92.0 0.0 copy-done.10
  92.0 1.2 convert_add_fusion
  93.3 0.0 copy-start.12
  93.3 2.1 %collective-permute-start.10 = (bf16[256,512]{1,0:T(8,128)(2,1)S(1)}, bf16[256,512]{1,0:T(8,128)(2,1)S(1)}, u32[]{:S(2)}, u32[]{:S(2)}) collective-permute-start(bf16[256,512]{1,0:T(8,128)(2,1)S(1)} %slice.91), channel_id=1, source_target_pairs={{0,2},{1,3},{2,0},{3,1},{4,6},{5,7},{6,4},{7,5},{8,10},{9,11},{10,... | collective-permute-start | bytes 786440 | tf_op jit(solution)/shard_map/ppermute | solution.py:208
  95.4 0.0 collective-permute-done.3
  95.4 0.1 fusion.3
  95.5 0.1 dynamic_update_slice.15
  95.5 0.0 collective-permute-done.8.held_ref
  95.6 4.9 %shard_map.93 = (f32[3,512,512]{2,1,0:T(8,128)S(1)}, bf16[96,1024]{1,0:T(8,128)(2,1)S(1)}, bf16[96,1024]{1,0:T(8,128)(2,1)S(1)}, bf16[96,1024]{1,0:T(8,128)(2,1)...) custom-call(bf16[3,512,512]{2,1,0:T(8,128)(2,1)} %collective-permute-done.8.held_ref,, ...), custom_call_target="tpu_custom_call" | custom-call | flops 1744830464 | bytes 4194304 | tf_op jit(solution)/shard_map/pallas_call | solution.py:186
  100.5 0.0 copy-done.12
  100.5 0.0 slice-start
  100.5 3.6 %shard_map.94 = f32[1,1,3,512,512]{4,3,2,1,0:T(8,128)} custom-call(f32[3,512,512]{2,1,0:T(8,128)S(1)} %get-tuple-element.31.old_ref, bf16[4,256,512]{2,1,0:T(8,128)(2,1)S(1)} %copy-done, bf16[4,256,512]{2,1,0:T(8,128)(2,1)S(1)} %copy-done.1, f32[3,256,1]{2,1,0:T(8,128)S(1)} %copy.11.rate_ref), custom_call_target="tpu_custom_call" | custom-call | flops 805306368 | bytes 4194304 | tf_op jit(solution)/shard_map/pallas_call | solution.py:186
  104.1 2.5 %collective-permute-start.15 = (bf16[64,1024]{1,0:T(8,128)(2,1)S(1)}, bf16[64,1024]{1,0:T(8,128)(2,1)S(1)}, u32[]{:S(2)}, u32[]{:S(2)}) collective-permute-start(bf16[64,1024]{1,0:T(8,128)(2,1)S(1)} %get-tuple-element.38), channel_id=1, source_target_pairs={{0,1},{1,0},{2,3},{3,2},{4,5},{5,4},{6,7},{7,6},{8,9},{9,8},{10,11... | collective-permute-start | bytes 393224 | tf_op jit(solution)/shard_map/ppermute | solution.py:200
  106.6 0.0 collective-permute-start.11
  106.6 2.0 %collective-permute-start.13 = (bf16[96,1024]{1,0:T(8,128)(2,1)S(1)}, bf16[96,1024]{1,0:T(8,128)(2,1)S(1)}, u32[]{:S(2)}, u32[]{:S(2)}) collective-permute-start(bf16[96,1024]{1,0:T(8,128)(2,1)S(1)} %get-tuple-element.36), channel_id=1, source_target_pairs={{0,1},{1,0},{2,3},{3,2},{4,5},{5,4},{6,7},{7,6},{8,9},{9,8},{10,11... | collective-permute-start | bytes 589832 | tf_op jit(solution)/shard_map/ppermute | solution.py:200
  108.6 0.0 collective-permute-done.10
  108.6 0.1 fusion.2
  108.7 2.4 %collective-permute-done.15 = bf16[64,1024]{1,0:T(8,128)(2,1)S(1)} collective-permute-done((bf16[64,1024]{1,0:T(8,128)(2,1)S(1)}, bf16[64,1024]{1,0:T(8,128)(2,1)S(1)}, u32[]{:S(2)}, u32[]{:S(2)}) %collective-permute-start.15) | collective-permute-done | bytes 131104 | tf_op jit(solution)/shard_map/ppermute | solution.py:200
  111.2 0.8 collective-permute-start.16
  112.0 4.8 %collective-permute-done.11 = bf16[96,1024]{1,0:T(8,128)(2,1)S(1)} collective-permute-done((bf16[96,1024]{1,0:T(8,128)(2,1)S(1)}, bf16[96,1024]{1,0:T(8,128)(2,1)S(1)}, u32[]{:S(2)}, u32[]{:S(2)}) %collective-permute-start.11) | collective-permute-done | bytes 196640 | tf_op jit(solution)/shard_map/ppermute | solution.py:200
  116.8 0.7 collective-permute-start.12
  117.5 3.4 %collective-permute-done.13 = bf16[96,1024]{1,0:T(8,128)(2,1)S(1)} collective-permute-done((bf16[96,1024]{1,0:T(8,128)(2,1)S(1)}, bf16[96,1024]{1,0:T(8,128)(2,1)S(1)}, u32[]{:S(2)}, u32[]{:S(2)}) %collective-permute-start.13) | collective-permute-done | bytes 196640 | tf_op jit(solution)/shard_map/ppermute | solution.py:200
  121.0 0.9 collective-permute-start.14
  122.0 2.5 %collective-permute-done.12 = bf16[96,512]{1,0:T(8,128)(2,1)S(1)} collective-permute-done((bf16[96,512]{1,0:T(8,128)(2,1)S(1)}, bf16[96,512]{1,0:T(8,128)(2,1)S(1)}, u32[]{:S(2)}, u32[]{:S(2)}) %collective-permute-start.12) | collective-permute-done | bytes 98336 | tf_op jit(solution)/shard_map/ppermute | solution.py:208
  124.5 4.3 %collective-permute-done.14 = bf16[96,512]{1,0:T(8,128)(2,1)S(1)} collective-permute-done((bf16[96,512]{1,0:T(8,128)(2,1)S(1)}, bf16[96,512]{1,0:T(8,128)(2,1)S(1)}, u32[]{:S(2)}, u32[]{:S(2)}) %collective-permute-start.14) | collective-permute-done | bytes 98336 | tf_op jit(solution)/shard_map/ppermute | solution.py:208
  128.9 0.0 collective-permute-done.16
  128.9 0.0 copy-start.13
  128.9 0.9 copy-done.13
  (30 shorter events, 0.3 us)
Async XLA Ops:
  0.6 8.0 %copy-start.1 = (bf16[4,256,512]{2,1,0:T(8,128)(2,1)S(1)}, bf16[4,256,512]{2,1,0:T(8,128)(2,1)}, u32[]{:S(2)}) copy-start(bf16[4,256,512]{2,1,0:T(8,128)(2,1)} %val_ref.3) | copy-start | bytes 3145732
  0.6 8.0 %copy-start = (bf16[4,256,512]{2,1,0:T(8,128)(2,1)S(1)}, bf16[4,256,512]{2,1,0:T(8,128)(2,1)}, u32[]{:S(2)}) copy-start(bf16[4,256,512]{2,1,0:T(8,128)(2,1)} %key_ref.3) | copy-start | bytes 3145732
  0.7 7.8 %copy-start.14 = (f32[3,256,1]{1,2,0:T(1,128)S(1)}, f32[3,256,1]{1,2,0:T(1,128)}, u32[]{:S(2)}) copy-start(f32[3,256,1]{1,2,0:T(1,128)} %param.10) | copy-start | bytes 9220
  2.8 52.6 %collective-permute-start = (bf16[2,256,512]{2,1,0:T(8,128)(2,1)}, bf16[2,256,512]{2,1,0:T(8,128)(2,1)}, u32[]{:S(2)}, u32[]{:S(2)}) collective-permute-start(bf16[2,256,512]{2,1,0:T(8,128)(2,1)} %get-tuple-element.21), channel_id=1, source_target_pairs={{0,4},{4,8},{8,12},{12,16},{16,20},{20,24},{24,28},{28,0},{1,5},{5... | collective-permute-start | bytes 1572872 | tf_op jit(solution)/shard_map/ppermute | solution.py:16
  3.3 13.7 %collective-permute-start.4 = (bf16[256,512]{1,0:T(8,128)(2,1)}, bf16[256,512]{1,0:T(8,128)(2,1)S(1)}, u32[]{:S(2)}, u32[]{:S(2)}) collective-permute-start(bf16[256,512]{1,0:T(8,128)(2,1)} %get-tuple-element.25), channel_id=1, source_target_pairs={{0,28},{4,0},{8,4},{12,8},{16,12},{20,16},{24,20},{28,24},{1,29},{... | collective-permute-start | bytes 786440 | tf_op jit(solution)/shard_map/ppermute | solution.py:16
  8.4 53.9 %collective-permute-start.6 = (bf16[2,256,512]{2,1,0:T(8,128)(2,1)}, bf16[2,256,512]{2,1,0:T(8,128)(2,1)}, u32[]{:S(2)}, u32[]{:S(2)}) collective-permute-start(bf16[2,256,512]{2,1,0:T(8,128)(2,1)} %get-tuple-element.26), channel_id=1, source_target_pairs={{0,4},{4,8},{8,12},{12,16},{16,20},{20,24},{24,28},{28,0},{1,5},{5... | collective-permute-start | bytes 1572872 | tf_op jit(solution)/shard_map/ppermute | solution.py:16
  8.6 1.9 %copy-start.2 = (f32[1,1,3,512,512]{4,3,2,1,0:T(8,128)S(1)}, f32[1,1,3,512,512]{4,3,2,1,0:T(8,128)}, u32[]{:S(2)}) copy-start(f32[1,1,3,512,512]{4,3,2,1,0:T(8,128)} %old_ref.3) | copy-start | bytes 9437188
  10.5 6.8 %copy-start.11 = (f32[512]{0:T(512)S(1)}, f32[512]{0:T(512)}, u32[]{:S(2)}) copy-start(f32[512]{0:T(512)} %param.11) | copy-start | bytes 6148
  10.5 44.9 %copy-start.3 = (f32[1,1,3,512,512]{4,3,2,1,0:T(8,128)S(1)}, f32[1,1,3,512,512]{4,3,2,1,0:T(8,128)}, u32[]{:S(2)}) copy-start(f32[1,1,3,512,512]{4,3,2,1,0:T(8,128)} %old_ref.3) | copy-start | bytes 9437188
  10.5 44.9 %copy-start.4 = (bf16[3,256,512]{2,1,0:T(8,128)(2,1)S(1)}, bf16[3,256,512]{2,1,0:T(8,128)(2,1)}, u32[]{:S(2)}) copy-start(bf16[3,256,512]{2,1,0:T(8,128)(2,1)} %q_ref.9) | copy-start | bytes 2359300
  10.5 44.9 %copy-start.5 = (bf16[512,2048]{1,0:T(8,128)(2,1)S(1)}, bf16[512,2048]{1,0:T(8,128)(2,1)}, u32[]{:S(2)}) copy-start(bf16[512,2048]{1,0:T(8,128)(2,1)} %w_ref.5) | copy-start | bytes 6291460
  13.5 82.1 %collective-permute-start.8 = (bf16[3,512,512]{2,1,0:T(8,128)(2,1)}, bf16[3,512,512]{2,1,0:T(8,128)(2,1)}, u32[]{:S(2)}, u32[]{:S(2)}) collective-permute-start(bf16[3,512,512]{2,1,0:T(8,128)(2,1)} %shard_map.88.held_ref), channel_id=1, source_target_pairs={{0,8},{4,12},{8,16},{12,20},{16,24},{20,28},{24,0},{28,4},{1,9},{5... | collective-permute-start | bytes 4718600 | tf_op jit(solution)/shard_map/ppermute | solution.py:16
  14.8 40.6 %collective-permute-start.1 = (f32[1,256]{1,0:T(1,128)S(1)}, f32[1,256]{1,0:T(1,128)S(1)}, u32[]{:S(2)}, u32[]{:S(2)}) collective-permute-start(f32[1,256]{1,0:T(1,128)S(1)} %slice_bitcast_fusion), channel_id=1, source_target_pairs={{0,4},{4,8},{8,12},{12,16},{16,20},{20,24},{24,28},{28,0},{1,5},{5... | collective-permute-start | bytes 3080 | tf_op jit(solution)/shard_map/ppermute | solution.py:16
  17.0 53.3 %collective-permute-start.9 = (bf16[2,256,512]{2,1,0:T(8,128)(2,1)}, bf16[2,256,512]{2,1,0:T(8,128)(2,1)}, u32[]{:S(2)}, u32[]{:S(2)}) collective-permute-start(bf16[2,256,512]{2,1,0:T(8,128)(2,1)} %get-tuple-element.29), channel_id=1, source_target_pairs={{0,4},{4,8},{8,12},{12,16},{16,20},{20,24},{24,28},{28,0},{1,5},{5... | collective-permute-start | bytes 1572872 | tf_op jit(solution)/shard_map/ppermute | solution.py:16
  55.4 8.4 %collective-permute-start.5 = (bf16[256,512]{1,0:T(8,128)(2,1)S(1)}, bf16[256,512]{1,0:T(8,128)(2,1)S(1)}, u32[]{:S(2)}, u32[]{:S(2)}) collective-permute-start(bf16[256,512]{1,0:T(8,128)(2,1)S(1)} %shard_map.89), channel_id=1, source_target_pairs={{0,4},{4,8},{8,12},{12,16},{16,20},{20,24},{24,28},{28,0},{1,5},{5... | collective-permute-start | bytes 786440 | tf_op jit(solution)/shard_map/ppermute | solution.py:16
  59.1 0.8 copy-start.7
  59.9 15.3 %collective-permute-start.2 = (bf16[256,1024]{1,0:T(8,128)(2,1)}, bf16[256,1024]{1,0:T(8,128)(2,1)}, u32[]{:S(2)}, u32[]{:S(2)}) collective-permute-start(bf16[256,1024]{1,0:T(8,128)(2,1)} %get-tuple-element.24), channel_id=1, source_target_pairs={{0,1},{1,0},{2,3},{3,2},{4,5},{5,4},{6,7},{7,6},{8,9},{9,8},{10,11... | collective-permute-start | bytes 1572872 | tf_op jit(solution)/shard_map/ppermute | solution.py:200
  67.1 0.8 copy-start.9
  67.9 24.2 %collective-permute-start.7 = (bf16[256,1024]{1,0:T(8,128)(2,1)}, bf16[256,1024]{1,0:T(8,128)(2,1)}, u32[]{:S(2)}, u32[]{:S(2)}) collective-permute-start(bf16[256,1024]{1,0:T(8,128)(2,1)} %get-tuple-element.28), channel_id=1, source_target_pairs={{0,1},{1,0},{2,3},{3,2},{4,5},{5,4},{6,7},{7,6},{8,9},{9,8},{10,11... | collective-permute-start | bytes 1572872 | tf_op jit(solution)/shard_map/ppermute | solution.py:200
  70.3 4.9 %copy-start.8 = (bf16[256,1024]{1,0:T(8,128)(2,1)S(1)}, bf16[256,1024]{1,0:T(8,128)(2,1)}, u32[]{:S(2)}) copy-start(bf16[256,1024]{1,0:T(8,128)(2,1)} %copy-done.7) | copy-start | bytes 1572868
  70.3 21.7 %copy-start.10 = (bf16[256,1024]{1,0:T(8,128)(2,1)S(1)}, bf16[256,1024]{1,0:T(8,128)(2,1)}, u32[]{:S(2)}) copy-start(bf16[256,1024]{1,0:T(8,128)(2,1)} %copy-done.9) | copy-start | bytes 1572868
  76.4 19.1 %copy-start.6 = (bf16[512,2048]{1,0:T(8,128)(2,1)S(1)}, bf16[512,2048]{1,0:T(8,128)(2,1)}, u32[]{:S(2)}) copy-start(bf16[512,2048]{1,0:T(8,128)(2,1)} %w_ref.5) | copy-start | bytes 6291460
  76.5 18.9 %collective-permute-start.3 = (bf16[256,512]{1,0:T(8,128)(2,1)S(1)}, bf16[256,512]{1,0:T(8,128)(2,1)S(1)}, u32[]{:S(2)}, u32[]{:S(2)}) collective-permute-start(bf16[256,512]{1,0:T(8,128)(2,1)S(1)} %slice.92), channel_id=1, source_target_pairs={{0,2},{1,3},{2,0},{3,1},{4,6},{5,7},{6,4},{7,5},{8,10},{9,11},{10,... | collective-permute-start | bytes 786440 | tf_op jit(solution)/shard_map/ppermute | solution.py:208
  93.3 7.2 %copy-start.12 = (f32[256,1024]{1,0:T(8,128)}, f32[256,1024]{1,0:T(8,128)S(1)}, u32[]{:S(2)}) copy-start(f32[256,1024]{1,0:T(8,128)S(1)} %convert_add_fusion) | copy-start | bytes 3145732
  93.3 15.3 %collective-permute-start.10 = (bf16[256,512]{1,0:T(8,128)(2,1)S(1)}, bf16[256,512]{1,0:T(8,128)(2,1)S(1)}, u32[]{:S(2)}, u32[]{:S(2)}) collective-permute-start(bf16[256,512]{1,0:T(8,128)(2,1)S(1)} %slice.91), channel_id=1, source_target_pairs={{0,2},{1,3},{2,0},{3,1},{4,6},{5,7},{6,4},{7,5},{8,10},{9,11},{10,... | collective-permute-start | bytes 786440 | tf_op jit(solution)/shard_map/ppermute | solution.py:208
  100.5 8.1 %slice-start = ((f32[256,1024]{1,0:T(8,128)}), f32[256,512]{1,0:T(8,128)S(1)}, s32[]{:S(2)}) async-start(f32[256,1024]{1,0:T(8,128)} %copy-done.12), calls=%async_computation | async-start | bytes 1048576 | tf_op jit(solution)/shard_map/slice | solution.py:203
  104.1 7.0 %collective-permute-start.15 = (bf16[64,1024]{1,0:T(8,128)(2,1)S(1)}, bf16[64,1024]{1,0:T(8,128)(2,1)S(1)}, u32[]{:S(2)}, u32[]{:S(2)}) collective-permute-start(bf16[64,1024]{1,0:T(8,128)(2,1)S(1)} %get-tuple-element.38), channel_id=1, source_target_pairs={{0,1},{1,0},{2,3},{3,2},{4,5},{5,4},{6,7},{7,6},{8,9},{9,8},{10,11... | collective-permute-start | bytes 393224 | tf_op jit(solution)/shard_map/ppermute | solution.py:200
  106.6 10.1 %collective-permute-start.11 = (bf16[96,1024]{1,0:T(8,128)(2,1)S(1)}, bf16[96,1024]{1,0:T(8,128)(2,1)S(1)}, u32[]{:S(2)}, u32[]{:S(2)}) collective-permute-start(bf16[96,1024]{1,0:T(8,128)(2,1)S(1)} %get-tuple-element.34), channel_id=1, source_target_pairs={{0,1},{1,0},{2,3},{3,2},{4,5},{5,4},{6,7},{7,6},{8,9},{9,8},{10,11... | collective-permute-start | bytes 589832 | tf_op jit(solution)/shard_map/ppermute | solution.py:200
  106.6 14.3 %collective-permute-start.13 = (bf16[96,1024]{1,0:T(8,128)(2,1)S(1)}, bf16[96,1024]{1,0:T(8,128)(2,1)S(1)}, u32[]{:S(2)}, u32[]{:S(2)}) collective-permute-start(bf16[96,1024]{1,0:T(8,128)(2,1)S(1)} %get-tuple-element.36), channel_id=1, source_target_pairs={{0,1},{1,0},{2,3},{3,2},{4,5},{5,4},{6,7},{7,6},{8,9},{9,8},{10,11... | collective-permute-start | bytes 589832 | tf_op jit(solution)/shard_map/ppermute | solution.py:200
  111.2 17.7 %collective-permute-start.16 = (bf16[64,512]{1,0:T(8,128)(2,1)S(1)}, bf16[64,512]{1,0:T(8,128)(2,1)S(1)}, u32[]{:S(2)}, u32[]{:S(2)}) collective-permute-start(bf16[64,512]{1,0:T(8,128)(2,1)S(1)} %slice.95), channel_id=1, source_target_pairs={{0,2},{1,3},{2,0},{3,1},{4,6},{5,7},{6,4},{7,5},{8,10},{9,11},{10,... | collective-permute-start | bytes 196616 | tf_op jit(solution)/shard_map/ppermute | solution.py:208
  116.8 7.7 %collective-permute-start.12 = (bf16[96,512]{1,0:T(8,128)(2,1)S(1)}, bf16[96,512]{1,0:T(8,128)(2,1)S(1)}, u32[]{:S(2)}, u32[]{:S(2)}) collective-permute-start(bf16[96,512]{1,0:T(8,128)(2,1)S(1)} %slice.94), channel_id=1, source_target_pairs={{0,2},{1,3},{2,0},{3,1},{4,6},{5,7},{6,4},{7,5},{8,10},{9,11},{10,... | collective-permute-start | bytes 294920 | tf_op jit(solution)/shard_map/ppermute | solution.py:208
  121.0 7.8 %collective-permute-start.14 = (bf16[96,512]{1,0:T(8,128)(2,1)S(1)}, bf16[96,512]{1,0:T(8,128)(2,1)S(1)}, u32[]{:S(2)}, u32[]{:S(2)}) collective-permute-start(bf16[96,512]{1,0:T(8,128)(2,1)S(1)} %slice.93), channel_id=1, source_target_pairs={{0,2},{1,3},{2,0},{3,1},{4,6},{5,7},{6,4},{7,5},{8,10},{9,11},{10,... | collective-permute-start | bytes 294920 | tf_op jit(solution)/shard_map/ppermute | solution.py:208
  128.9 0.9 copy-start.13
